TPU v7x, 128 devices: a whole 4x4x4 slice. The times are simulated.
128 devices in a mesh: gx: 16 (over x, y), gy: 8 (over z, core).
Axes of the slice: x: 4, y: 4, z: 4, core: 2. Of those that a mesh axis runs over, the one named last changes fastest.
Arguments:
- tensor: float32 [256, 512, 1024], P('gx', None, 'gy'), may hold values from -80 to 80
- start_basis: float32 [512, 384], replicated, may hold values from -6 to 6
Outputs:
- core: float32 [256, 384, 1024], P('gx', 'gy')
All inputs are finite; a program needn't handle non-finite values.
Results may differ from a plain program's by a relative error of at most 0.00019.
Values sent between devices are 32-bit elements; how exact they have to be, the bound alone decides.
A program may use at most 512 MiB of HBM per device.

v0:
```python
import jax
import jax.numpy as jnp
from jax import lax
from jax.sharding import PartitionSpec as P

ITERS = 2


def matmul(left, right):
    return jnp.dot(left, right, precision=lax.Precision.HIGHEST, preferred_element_type=jnp.float32)


def orthonormal(product):
    product_gram = matmul(product.T, product)
    lower = jnp.linalg.cholesky(product_gram)
    return jax.scipy.linalg.solve_triangular(lower, product.T, lower=True).T


def body(tensor, start_basis):
    local_gram = lax.dot_general(
        tensor,
        tensor,
        (((0, 2), (0, 2)), ((), ())),
        precision=lax.Precision.HIGHEST,
        preferred_element_type=jnp.float32,
    )
    gram = lax.psum(local_gram, ("gx", "gy"))
    basis = start_basis
    for sweep in range(ITERS):
        product = matmul(gram, basis)
        basis = orthonormal(product)
    core_local = jnp.einsum(
        "ar,kac->krc",
        basis,
        tensor,
        precision=lax.Precision.HIGHEST,
        preferred_element_type=jnp.float32,
    )
    return lax.all_to_all(core_local, "gy", split_axis=1, concat_axis=2, tiled=True)


def solution(mesh):
    placed = (P("gx", None, "gy"), P())
    return jax.shard_map(
        body, mesh=mesh, in_specs=placed, out_specs=P("gx", "gy", None), check_vma=False
    )
```

profile of v0, /device:TPU:1, one launch (start us, length us, event | category | flops | bytes accessed | tf_op | source)
XLA Modules:
  0.0 449.4 jit_solution(3196692239382905080)
XLA Ops:
  6.5 11.5 %convolution_bitcast_fusion.1 = f32[512,512]{1,0:T(8,128)} fusion(f32[16,512,128]{2,1,0:T(8,128)} %param.5), kind=kOutput, calls=%fused_computation.5 | convolution fusion | flops 6442450944 | bytes 5242880 | tf_op jit(solution)/shard_map/dot_general | solution.py:20
  18.1 150.7 %all-reduce.3.cloned.1.call-done = f32[512,512]{1,0:T(8,128)} async-done(((f32[512,512]{1,0:T(8,128)}), f32[512,512]{1,0:T(8,128)}) %all-reduce.3.cloned.1.call-update) | async-done | bytes 1048592 | tf_op jit(solution)/shard_map/psum | solution.py:27
  168.8 3.0 fusion.56
  171.8 1.4 fusion.57
  174.4 11.7 %cholesky.208 = f32[128,128]{1,0:T(8,128)S(1)} custom-call(f32[128,128]{1,0:T(8,128)S(1)} %cholesky.310), custom_call_target="Cholesky" | custom-call | tf_op jit(solution)/shard_map/jit(cholesky)/cholesky | solution.py:15
  186.1 9.8 %custom-call.20 = f32[1,128,128]{1,2,0:T(8,128)S(1)} custom-call(f32[1,128,128]{2,1,0:T(8,128)S(1)} %get-tuple-element.56), custom_call_target="InvertDiagBlocksLowerTriangular" | custom-call | tf_op jit(solution)/shard_map/jit(cholesky)/cholesky | solution.py:15
  198.5 12.1 %cholesky.227 = f32[128,128]{1,0:T(8,128)S(1)} custom-call(f32[128,128]{1,0:T(8,128)S(1)} %cholesky.314), custom_call_target="Cholesky" | custom-call | tf_op jit(solution)/shard_map/jit(cholesky)/cholesky | solution.py:15
  210.6 9.8 %custom-call.21 = f32[1,128,128]{1,2,0:T(8,128)S(1)} custom-call(f32[1,128,128]{2,1,0:T(8,128)S(1)} %get-tuple-element.53), custom_call_target="InvertDiagBlocksLowerTriangular" | custom-call | tf_op jit(solution)/shard_map/jit(cholesky)/cholesky | solution.py:15
  221.8 11.7 %cholesky.246 = f32[128,128]{1,0:T(8,128)S(1)} custom-call(f32[128,128]{1,0:T(8,128)S(1)} %convolution_subtract_fusion.7), custom_call_target="Cholesky" | custom-call | tf_op jit(solution)/shard_map/jit(cholesky)/cholesky | solution.py:15
  237.7 8.7 %while.4 = (s32[]{:T(128)}, f32[384,384]{1,0:T(8,128)}, s32[3,2]{0,1:T(2,128)S(1)}, f32[3,128,128]{2,1,0:T(8,128)S(1)}, s32[]{:T(128)}) while((s32[]{:T(128)}, f32[384,384]{1,0:T(8,128)}, s32[3,2]{0,1:T(2,128)S(1)}, f32[3,128,128]{2,1,0:T(8,128)S(1)}, s32[]{:T(128)}) %tuple.47), condition=%wide.while_cond, body=%wide.while_body.sunk | while | flops 2 | bytes 131189 | solution.py:16
  238.3 2.3 bitcast_dynamic-update-slice_fusion.4
  241.3 2.3 bitcast_dynamic-update-slice_fusion.4
  244.2 2.2 bitcast_dynamic-update-slice_fusion.4
  246.4 29.7 %custom-call.22 = f32[3,128,128]{1,2,0:T(8,128)S(1)} custom-call(f32[3,128,128]{2,1,0:T(8,128)S(1)} %get-tuple-element.21), custom_call_target="InvertDiagBlocksLowerTriangular" | custom-call | tf_op jit(solution)/shard_map/jit(_solve_triangular)/triangular_solve | solution.py:16
  276.5 1.4 convolution_subtract_fusion.3
  278.4 1.9 convolution_subtract_fusion.2
  280.7 1.8 fusion
  282.6 1.4 fusion.58
  284.3 11.7 %cholesky.261 = f32[128,128]{1,0:T(8,128)S(1)} custom-call(f32[128,128]{1,0:T(8,128)S(1)} %cholesky.318), custom_call_target="Cholesky" | custom-call | tf_op jit(solution)/shard_map/jit(cholesky)/cholesky | solution.py:15
  296.7 10.0 %custom-call.23 = f32[1,128,128]{1,2,0:T(8,128)S(1)} custom-call(f32[1,128,128]{2,1,0:T(8,128)S(1)} %get-tuple-element.49), custom_call_target="InvertDiagBlocksLowerTriangular" | custom-call | tf_op jit(solution)/shard_map/jit(cholesky)/cholesky | solution.py:15
  307.3 11.7 %cholesky.280 = f32[128,128]{1,0:T(8,128)S(1)} custom-call(f32[128,128]{1,0:T(8,128)S(1)} %cholesky.322), custom_call_target="Cholesky" | custom-call | tf_op jit(solution)/shard_map/jit(cholesky)/cholesky | solution.py:15
  319.8 9.8 %custom-call.24 = f32[1,128,128]{1,2,0:T(8,128)S(1)} custom-call(f32[1,128,128]{2,1,0:T(8,128)S(1)} %get-tuple-element.46), custom_call_target="InvertDiagBlocksLowerTriangular" | custom-call | tf_op jit(solution)/shard_map/jit(cholesky)/cholesky | solution.py:15
  330.1 11.7 %cholesky.299 = f32[128,128]{1,0:T(8,128)S(1)} custom-call(f32[128,128]{1,0:T(8,128)S(1)} %convolution_subtract_fusion.6), custom_call_target="Cholesky" | custom-call | tf_op jit(solution)/shard_map/jit(cholesky)/cholesky | solution.py:15
  344.5 6.4 %while.5 = (s32[]{:T(128)}, f32[384,384]{1,0:T(8,128)S(1)}, s32[3,2]{0,1:T(2,128)S(1)}, f32[3,128,128]{2,1,0:T(8,128)S(1)}, s32[]{:T(128)}) while((s32[]{:T(128)}, f32[384,384]{1,0:T(8,128)S(1)}, s32[3,2]{0,1:T(2,128)S(1)}, f32[3,128,128]{2,1,0:T(8,128)S(1)}, s32[]{:T(128)}) %tuple.55), condition=%wide.while_cond.clone, body=%wide.while_body.clone.sunk | while | flops 2 | bytes 131189 | solution.py:16
  345.2 1.4 bitcast_dynamic-update-slice_fusion.5
  347.3 1.4 bitcast_dynamic-update-slice_fusion.5
  350.8 29.7 %custom-call.25 = f32[3,128,128]{1,2,0:T(8,128)S(1)} custom-call(f32[3,128,128]{2,1,0:T(8,128)S(1)} %get-tuple-element.22), custom_call_target="InvertDiagBlocksLowerTriangular" | custom-call | tf_op jit(solution)/shard_map/jit(_solve_triangular)/triangular_solve | solution.py:16
  383.5 7.1 %convolution_bitcast_fusion = f32[16,384,128]{2,1,0:T(8,128)S(1)} fusion(f32[16,512,128]{2,1,0:T(8,128)} %param.5, f32[128,512]{1,0:T(8,128)S(1)} %fusion.30, f32[128,512]{1,0:T(8,128)S(1)} %fusion.32, f32[128,512]{1,0:T(8,128)S(1)} %fusion.18), kind=kOutput, calls=%fused_computation.4 | convolution fusion | flops 4832231424 | bytes 8126464 | tf_op jit(solution)/shard_map/ar,kac->krc/dot_general | solution.py:32
  390.6 1.8 copy.8
  392.4 41.7 %all_to_all.18 = f32[16,384,128]{2,0,1:T(8,128)S(1)} all-to-all(f32[16,384,128]{2,0,1:T(8,128)S(1)} %copy.8), channel_id=1, replica_groups=mesh['gx'=16,'gy'=8] {'gy'}, dimensions={1} | all-to-all | bytes 6291456 | tf_op jit(solution)/shard_map/all_to_all | solution.py:39
  434.1 3.5 copy.9
  437.6 4.5 %all_to_all.16 = f32[16,48,1024]{2,1,0:T(8,128)} reshape(f32[16,48,8,128]{3,2,1,0:T(8,128)} %copy.9) | data formatting | bytes 6291456 | tf_op jit(solution)/shard_map/all_to_all | solution.py:39
  (64 shorter events, 20.3 us)
Async XLA Ops:
  6.5 162.3 %copy-start = (f32[512,384]{1,0:T(8,128)S(1)}, f32[512,384]{1,0:T(8,128)}, u32[]{:S(2)}) copy-start(f32[512,384]{1,0:T(8,128)} %param.6) | copy-start | bytes 2359300
  6.5 162.3 %all-reduce.3.cloned.1.call-start = ((), (), s32[]{:S(2)}) async-start(), calls=%async_computation.1 | async-start | bytes 2097152 | tf_op jit(solution)/shard_map/psum | solution.py:27
  173.6 0.8 copy-start.2
  196.0 84.8 %copy-start.1 = (f32[512,512]{1,0:T(8,128)S(1)}, f32[512,512]{1,0:T(8,128)}, u32[]{:S(2)}) copy-start(f32[512,512]{1,0:T(8,128)} %all-reduce.3.cloned.1.call-done) | copy-start | bytes 3145732
Sparse Core Ops, SparseCore 0:
  18.2 150.5 all-reduce.2
where the time goes:
time: 453 us; the launch traced here: 449 us
  other arithmetic  174 us (38%)
  waiting for transfers between devices  151 us (33%)
  blocking collectives  41.7 us (9%)
  matrix products  38.5 us (8%)
  local copies, waits for them, and re-layouts  26.2 us (6%)
  between operations  18 us (4%)
    psum x1, waiting for transfers between devices, body(): gram = lax.psum(local_gram, ('gx', 'gy'))  151 us
    another operation x21, other arithmetic, orthonormal(): lower = jnp.linalg.cholesky(product_gram)  114 us
    another operation x5, other arithmetic, orthonormal(): return jax.scipy.linalg.solve_triangular(lower, product.T, lower=True).T  60.3 us
    all_to_all x1, blocking collectives, body(): lax.all_to_all(core_local, 'gy', split_axis=1, concat_axis=2, tiled=True)  41.7 us
    another operation x21, local copies, waits for them, and re-layouts, orthonormal(): return jax.scipy.linalg.solve_triangular(lower, product.T, lower=True).T  15 us
    dot_general x1, matrix products, body(): lax.dot_general(tensor, tensor, (((0, 2), (0, 2)), ((), ())), precision=l...  11.5 us
  transfers between devices with their start and end apart: 1, of which 1 were waited for; matrix products, arithmetic and copies ran while one was open for 0% of the time, Pallas kernels for 0%

commit v1 on v0

--- a/solution.py
+++ b/solution.py
@@ -24,7 +24,7 @@
         precision=lax.Precision.HIGHEST,
         preferred_element_type=jnp.float32,
     )
-    gram = lax.psum(local_gram, ("gx", "gy"))
+    gram = lax.psum(lax.psum(local_gram, "gy"), "gx")
     basis = start_basis
     for sweep in range(ITERS):
         product = matmul(gram, basis)

time: 453 us -> 462 us (1.020)
    psum x1 -> x2, waiting for transfers between devices: 151 us -> 154 us  [body(): gram = lax.psum(lax.psum(local_gram, 'gy'), 'gx')]
  transfers between devices with their start and end apart: 1 -> 2, of which waited for: 1 -> 2; matrix products, arithmetic and copies ran while one was open for 0% -> 0% of each run, Pallas kernels for 0% -> 0%
where the time goes in v1:
time: 462 us; the launch traced here: 458 us
  other arithmetic  174 us (38%)
  waiting for transfers between devices  154 us (33%)
  blocking collectives  44.3 us (10%)
  matrix products  40.9 us (9%)
  local copies, waits for them, and re-layouts  27.1 us (6%)
  between operations  18 us (4%)
    psum x2, waiting for transfers between devices, body(): gram = lax.psum(lax.psum(local_gram, 'gy'), 'gx')  154 us
    another operation x21, other arithmetic, orthonormal(): lower = jnp.linalg.cholesky(product_gram)  114 us
    another operation x5, other arithmetic, orthonormal(): return jax.scipy.linalg.solve_triangular(lower, product.T, lower=True).T  60.3 us
    all_to_all x1, blocking collectives, body(): lax.all_to_all(core_local, 'gy', split_axis=1, concat_axis=2, tiled=True)  44.3 us
    another operation x21, local copies, waits for them, and re-layouts, orthonormal(): return jax.scipy.linalg.solve_triangular(lower, product.T, lower=True).T  15 us
    dot_general x1, matrix products, body(): lax.dot_general(tensor, tensor, (((0, 2), (0, 2)), ((), ())), precision=l...  11.3 us
  transfers between devices with their start and end apart: 2, of which 2 were waited for; matrix products, arithmetic and copies ran while one was open for 0% of the time, Pallas kernels for 0%

profile of v1, /device:TPU:1, one launch (start us, length us, event | category | flops | bytes accessed | tf_op | source)
XLA Modules:
  0.0 458.4 jit_solution(1013227493495849569)
XLA Ops:
  6.5 11.3 %convolution_bitcast_fusion.1 = f32[512,512]{1,0:T(8,128)} fusion(f32[16,512,128]{2,1,0:T(8,128)} %param.5), kind=kOutput, calls=%fused_computation.5 | convolution fusion | flops 6442450944 | bytes 5242880 | tf_op jit(solution)/shard_map/dot_general | solution.py:20
  18.1 63.8 %all-reduce.4.cloned.1.call-done = f32[512,512]{1,0:T(8,128)} async-done(((f32[512,512]{1,0:T(8,128)}), f32[512,512]{1,0:T(8,128)}) %all-reduce.4.cloned.1.call-update) | async-done | bytes 1048592 | tf_op jit(solution)/shard_map/psum | solution.py:27
  81.9 89.8 %all-reduce.6.cloned.1.call-done = f32[512,512]{1,0:T(8,128)} async-done(((f32[512,512]{1,0:T(8,128)}), f32[512,512]{1,0:T(8,128)}) %all-reduce.6.cloned.1.call-update) | async-done | bytes 1048592 | tf_op jit(solution)/shard_map/psum | solution.py:27
  171.7 3.0 fusion.56
  174.8 1.4 fusion.57
  177.3 11.7 %cholesky.208 = f32[128,128]{1,0:T(8,128)S(1)} custom-call(f32[128,128]{1,0:T(8,128)S(1)} %cholesky.310), custom_call_target="Cholesky" | custom-call | tf_op jit(solution)/shard_map/jit(cholesky)/cholesky | solution.py:15
  189.1 9.8 %custom-call.20 = f32[1,128,128]{1,2,0:T(8,128)S(1)} custom-call(f32[1,128,128]{2,1,0:T(8,128)S(1)} %get-tuple-element.56), custom_call_target="InvertDiagBlocksLowerTriangular" | custom-call | tf_op jit(solution)/shard_map/jit(cholesky)/cholesky | solution.py:15
  201.4 12.1 %cholesky.227 = f32[128,128]{1,0:T(8,128)S(1)} custom-call(f32[128,128]{1,0:T(8,128)S(1)} %cholesky.314), custom_call_target="Cholesky" | custom-call | tf_op jit(solution)/shard_map/jit(cholesky)/cholesky | solution.py:15
  213.5 9.8 %custom-call.21 = f32[1,128,128]{1,2,0:T(8,128)S(1)} custom-call(f32[1,128,128]{2,1,0:T(8,128)S(1)} %get-tuple-element.53), custom_call_target="InvertDiagBlocksLowerTriangular" | custom-call | tf_op jit(solution)/shard_map/jit(cholesky)/cholesky | solution.py:15
  224.7 11.7 %cholesky.246 = f32[128,128]{1,0:T(8,128)S(1)} custom-call(f32[128,128]{1,0:T(8,128)S(1)} %convolution_subtract_fusion.7), custom_call_target="Cholesky" | custom-call | tf_op jit(solution)/shard_map/jit(cholesky)/cholesky | solution.py:15
  240.6 8.8 %while.4 = (s32[]{:T(128)}, f32[384,384]{1,0:T(8,128)}, s32[3,2]{0,1:T(2,128)S(1)}, f32[3,128,128]{2,1,0:T(8,128)S(1)}, s32[]{:T(128)}) while((s32[]{:T(128)}, f32[384,384]{1,0:T(8,128)}, s32[3,2]{0,1:T(2,128)S(1)}, f32[3,128,128]{2,1,0:T(8,128)S(1)}, s32[]{:T(128)}) %tuple.47), condition=%wide.while_cond, body=%wide.while_body.sunk | while | flops 2 | bytes 131189 | solution.py:16
  241.3 2.3 bitcast_dynamic-update-slice_fusion.4
  244.2 2.3 bitcast_dynamic-update-slice_fusion.4
  247.2 2.2 bitcast_dynamic-update-slice_fusion.4
  249.4 29.7 %custom-call.22 = f32[3,128,128]{1,2,0:T(8,128)S(1)} custom-call(f32[3,128,128]{2,1,0:T(8,128)S(1)} %get-tuple-element.21), custom_call_target="InvertDiagBlocksLowerTriangular" | custom-call | tf_op jit(solution)/shard_map/jit(_solve_triangular)/triangular_solve | solution.py:16
  279.5 1.4 convolution_subtract_fusion.3
  281.3 1.9 convolution_subtract_fusion.2
  283.7 1.8 fusion
  285.5 1.4 fusion.58
  288.1 11.7 %cholesky.261 = f32[128,128]{1,0:T(8,128)S(1)} custom-call(f32[128,128]{1,0:T(8,128)S(1)} %cholesky.318), custom_call_target="Cholesky" | custom-call | tf_op jit(solution)/shard_map/jit(cholesky)/cholesky | solution.py:15
  300.5 10.0 %custom-call.23 = f32[1,128,128]{1,2,0:T(8,128)S(1)} custom-call(f32[1,128,128]{2,1,0:T(8,128)S(1)} %get-tuple-element.49), custom_call_target="InvertDiagBlocksLowerTriangular" | custom-call | tf_op jit(solution)/shard_map/jit(cholesky)/cholesky | solution.py:15
  312.9 11.7 %cholesky.280 = f32[128,128]{1,0:T(8,128)S(1)} custom-call(f32[128,128]{1,0:T(8,128)S(1)} %cholesky.322), custom_call_target="Cholesky" | custom-call | tf_op jit(solution)/shard_map/jit(cholesky)/cholesky | solution.py:15
  325.3 9.8 %custom-call.24 = f32[1,128,128]{1,2,0:T(8,128)S(1)} custom-call(f32[1,128,128]{2,1,0:T(8,128)S(1)} %get-tuple-element.46), custom_call_target="InvertDiagBlocksLowerTriangular" | custom-call | tf_op jit(solution)/shard_map/jit(cholesky)/cholesky | solution.py:15
  336.5 11.7 %cholesky.299 = f32[128,128]{1,0:T(8,128)S(1)} custom-call(f32[128,128]{1,0:T(8,128)S(1)} %convolution_subtract_fusion.6), custom_call_target="Cholesky" | custom-call | tf_op jit(solution)/shard_map/jit(cholesky)/cholesky | solution.py:15
  350.8 6.4 %while.5 = (s32[]{:T(128)}, f32[384,384]{1,0:T(8,128)S(1)}, s32[3,2]{0,1:T(2,128)S(1)}, f32[3,128,128]{2,1,0:T(8,128)S(1)}, s32[]{:T(128)}) while((s32[]{:T(128)}, f32[384,384]{1,0:T(8,128)S(1)}, s32[3,2]{0,1:T(2,128)S(1)}, f32[3,128,128]{2,1,0:T(8,128)S(1)}, s32[]{:T(128)}) %tuple.57), condition=%wide.while_cond.clone, body=%wide.while_body.clone.sunk | while | flops 2 | bytes 131189 | solution.py:16
  351.5 1.4 bitcast_dynamic-update-slice_fusion.5
  357.2 29.7 %custom-call.25 = f32[3,128,128]{1,2,0:T(8,128)S(1)} custom-call(f32[3,128,128]{2,1,0:T(8,128)S(1)} %get-tuple-element.22), custom_call_target="InvertDiagBlocksLowerTriangular" | custom-call | tf_op jit(solution)/shard_map/jit(_solve_triangular)/triangular_solve | solution.py:16
  389.8 7.1 %convolution_bitcast_fusion = f32[16,384,128]{2,1,0:T(8,128)S(1)} fusion(f32[16,512,128]{2,1,0:T(8,128)} %param.5, f32[128,512]{1,0:T(8,128)S(1)} %fusion.30, f32[128,512]{1,0:T(8,128)S(1)} %fusion.32, f32[128,512]{1,0:T(8,128)S(1)} %fusion.18), kind=kOutput, calls=%fused_computation.4 | convolution fusion | flops 4832231424 | bytes 8126464 | tf_op jit(solution)/shard_map/ar,kac->krc/dot_general | solution.py:32
  396.9 1.8 copy.8
  398.8 44.3 %all_to_all.18 = f32[16,384,128]{2,0,1:T(8,128)S(1)} all-to-all(f32[16,384,128]{2,0,1:T(8,128)S(1)} %copy.8), channel_id=1, replica_groups=mesh['gx'=16,'gy'=8] {'gy'}, dimensions={1} | all-to-all | bytes 6291456 | tf_op jit(solution)/shard_map/all_to_all | solution.py:39
  443.1 3.5 copy.9
  446.5 4.5 all_to_all.16
  (69 shorter events, 25.5 us)
Async XLA Ops:
  6.5 165.2 %copy-start = (f32[512,384]{1,0:T(8,128)S(1)}, f32[512,384]{1,0:T(8,128)}, u32[]{:S(2)}) copy-start(f32[512,384]{1,0:T(8,128)} %param.6) | copy-start | bytes 2359300
  6.5 75.4 %all-reduce.4.cloned.1.call-start = ((), (), s32[]{:S(2)}) async-start(), calls=%async_computation.1 | async-start | bytes 2097152 | tf_op jit(solution)/shard_map/psum | solution.py:27
  17.9 153.9 %all-reduce.6.cloned.1.call-start = ((), (), s32[]{:S(2)}) async-start(), calls=%async_computation.2 | async-start | bytes 2097152 | tf_op jit(solution)/shard_map/psum | solution.py:27
  176.5 0.8 copy-start.3
  198.9 84.7 %copy-start.1 = (f32[512,512]{1,0:T(8,128)S(1)}, f32[512,512]{1,0:T(8,128)}, u32[]{:S(2)}) copy-start(f32[512,512]{1,0:T(8,128)} %all-reduce.6.cloned.1.call-done) | copy-start | bytes 3145732
  287.2 0.8 copy-start.2
Sparse Core Ops, SparseCore 0:
  18.0 63.8 all-reduce.3
  85.1 86.5 all-reduce.5
